TPU v7x, 32 devices: a whole 2x2x4 slice. The times are simulated.
32 devices in a mesh: row: 8 (over z, x), col: 4 (over y, core).
Axes of the slice: x: 2, y: 2, z: 4, core: 2. Of those that a mesh axis runs over, the one named last changes fastest.
Arguments:
- alignment: bfloat16 [256, 192, 256], P('row', 'col'), may hold values from -8 to 8
- alignment_mask: int32 [256, 192], P('row', 'col'), may hold values from 0 to 1, as said below
- residue_mask: int32 [192], replicated, may hold values from 0 to 1, as said below
- pair_features: bfloat16 [192, 192, 128], P('row', 'col'), may hold values from -6 to 6
- outer_product_left: bfloat16 [256, 32], replicated, may hold values from -0.375 to 0.375
- outer_product_right: bfloat16 [256, 32], replicated, may hold values from -0.375 to 0.375
- outer_proj: bfloat16 [1024, 128], replicated, may hold values from -0.1875 to 0.1875
- triangle_proj: bfloat16 [128, 512], replicated, may hold values from -0.5 to 0.5
- triangle_gate: bfloat16 [128, 128], replicated, may hold values from -0.5 to 0.5
- triangle_out: bfloat16 [128, 128], replicated, may hold values from -0.5 to 0.5
- transition_in: bfloat16 [128, 512], replicated, may hold values from -0.5 to 0.5
- transition_out: bfloat16 [512, 128], replicated, may hold values from -0.25 to 0.25
Outputs:
- pair_out: bfloat16 [192, 192, 128], P('row', 'col')
Inputs may be any that keep to these rules, and one draw needn't show every extreme that they name: `residue_mask`: masked residues scattered anywhere; at least one residue is masked and at least one takes part. `alignment_mask`: 0 wherever residue_mask is 0.
All inputs are finite; a program needn't handle non-finite values.
Results may differ from a plain program's by a relative error of at most 0.014.
Values may be sent and summed in bfloat16 or wider, within the bound.
No kernel may reach another device: no remote copies, remote signals or barrier semaphores. Data moves between devices by JAX's collectives and lax.ppermute only.
A program may use at most 64 MiB of HBM per device.

v0:
```python
import jax
import jax.numpy as jnp
from jax import lax
from jax.sharding import PartitionSpec as P

epsilon = 1e-05


def normalize(values):
    mean_value = jnp.mean(values, axis=-1, keepdims=True)
    centered = values - mean_value
    variance = jnp.mean(centered * centered, axis=-1, keepdims=True)
    return centered * lax.rsqrt(variance + epsilon)


def shards(
    alignment,
    alignment_mask,
    residue_mask,
    pair_features,
    outer_product_left,
    outer_product_right,
    outer_proj,
    triangle_proj,
    triangle_gate,
    triangle_out,
    transition_in,
    transition_out,
):
    block_rows, block_cols, channels = pair_features.shape
    inner = triangle_out.shape[0]
    narrow = outer_product_left.shape[1]
    mask_float = alignment_mask.astype(jnp.float32)
    normed = normalize(alignment.astype(jnp.float32)).astype(jnp.bfloat16)
    left_side = (
        jnp.dot(normed, outer_product_left, preferred_element_type=jnp.float32)
        * mask_float[..., None]
    ).astype(jnp.bfloat16)
    right_side = (
        jnp.dot(normed, outer_product_right, preferred_element_type=jnp.float32)
        * mask_float[..., None]
    ).astype(jnp.bfloat16)
    mask_wire = alignment_mask.astype(jnp.bfloat16)
    right_all, right_mask = (
        lax.all_gather(right_side, "row", axis=0, tiled=True),
        lax.all_gather(mask_wire, "row", axis=0, tiled=True),
    )
    left_rows, left_row_mask = (
        lax.all_gather(left_side, "col", axis=1, tiled=True),
        lax.all_gather(mask_wire, "col", axis=1, tiled=True),
    )
    left_all, left_mask = (
        lax.all_to_all(left_rows, "row", split_axis=1, concat_axis=0, tiled=True),
        lax.all_to_all(left_row_mask, "row", split_axis=1, concat_axis=0, tiled=True),
    )
    sequences = left_all.shape[0]
    contract = (((0,), (0,)), ((), ()))
    outer = lax.dot_general(
        left_all.reshape(sequences, block_rows * narrow),
        right_all.reshape(sequences, block_cols * narrow),
        contract,
        preferred_element_type=jnp.float32,
    )
    outer = (
        outer.reshape(block_rows, narrow, block_cols, narrow)
        .transpose(0, 2, 1, 3)
        .astype(jnp.bfloat16)
    )
    outer = outer.reshape(block_rows, block_cols, narrow * narrow)
    projected = jnp.dot(outer, outer_proj, preferred_element_type=jnp.float32)
    counts = lax.dot_general(left_mask, right_mask, contract, preferred_element_type=jnp.float32)
    first = (
        pair_features.astype(jnp.float32) + projected / jnp.maximum(counts, 1.0)[..., None]
    ).astype(jnp.bfloat16)
    normed_pair = normalize(first.astype(jnp.float32)).astype(jnp.bfloat16)
    projections = jnp.dot(normed_pair, triangle_proj, preferred_element_type=jnp.float32)
    row_mask = lax.dynamic_slice_in_dim(
        residue_mask, lax.axis_index("row") * block_rows, block_rows
    ).astype(jnp.float32)
    col_mask = lax.dynamic_slice_in_dim(
        residue_mask, lax.axis_index("col") * block_cols, block_cols
    ).astype(jnp.float32)
    pair_mask = (row_mask[:, None] * col_mask[None, :])[..., None]
    left_tri = (
        jax.nn.sigmoid(projections[..., :inner]) * projections[..., inner : 2 * inner] * pair_mask
    ).astype(jnp.bfloat16)
    right_tri = (
        jax.nn.sigmoid(projections[..., 2 * inner : 3 * inner])
        * projections[..., 3 * inner :]
        * pair_mask
    ).astype(jnp.bfloat16)
    right_cols = lax.all_gather(right_tri, "row", axis=0, tiled=True)
    right_rows = lax.all_to_all(right_cols, "col", split_axis=0, concat_axis=1, tiled=True)
    summed = jnp.einsum(
        "ikc,jkc->ijc",
        lax.all_gather(left_tri, "col", axis=1, tiled=True),
        right_rows,
        preferred_element_type=jnp.float32,
    )
    normed_sum = normalize(summed).astype(jnp.bfloat16)
    update = jax.nn.sigmoid(
        jnp.dot(normed_pair, triangle_gate, preferred_element_type=jnp.float32)
    ) * jnp.dot(normed_sum, triangle_out, preferred_element_type=jnp.float32)
    second = (first.astype(jnp.float32) + update).astype(jnp.bfloat16)
    normed_second = normalize(second.astype(jnp.float32)).astype(jnp.bfloat16)
    hidden_units = jnp.maximum(
        jnp.dot(normed_second, transition_in, preferred_element_type=jnp.float32), 0.0
    ).astype(jnp.bfloat16)
    return (
        second.astype(jnp.float32)
        + jnp.dot(hidden_units, transition_out, preferred_element_type=jnp.float32)
    ).astype(jnp.bfloat16)


def solution(mesh):
    placed = (
        P("row", "col", None),
        P("row", "col"),
        P(),
        P("row", "col", None),
        P(),
        P(),
        P(),
        P(),
        P(),
        P(),
        P(),
        P(),
    )
    return jax.shard_map(
        shards, mesh=mesh, in_specs=placed, out_specs=P("row", "col", None), check_vma=False
    )
```

profile of v0, /device:TPU:0, one launch (start us, length us, event | category | flops | bytes accessed | tf_op | source)
XLA Modules:
  0.0 276.2 jit_solution(16021958013082864905)
XLA Ops:
  7.4 6.2 %all-gather = bf16[4,48,32]{1,2,0:T(8,128)(2,1)S(1)} all-gather(bf16[1,48,32]{1,2,0:T(8,128)(2,1)S(1)} %bitcast.93), channel_id=1, replica_groups=mesh['row'=8,'col'=4] {'col'}, dimensions={0}, use_global_device_ids=true | all-gather | bytes 15360 | tf_op jit(solution)/shard_map/all_gather | solution.py:50
  14.5 6.2 %all-to-all-start.1 = ((bf16[8,2,384]{2,1,0:T(2,128)(2,1)}), bf16[8,2,384]{2,1,0:T(2,128)(2,1)S(1)}, u32[]{:S(2)}, u32[]{:S(2)}) async-start(bf16[8,2,384]{2,1,0:T(2,128)(2,1)} %reshape.110), calls=%async_computation.1 | async-start | bytes 24576 | tf_op jit(solution)/shard_map/all_to_all | solution.py:54
  20.8 1.4 convert_reduce_fusion
  24.1 13.4 %all_gather.18 = bf16[32,192,32]{2,0,1:T(8,128)(2,1)} all-gather(bf16[32,48,32]{2,0,1:T(8,128)(2,1)S(1)} %copy.51), channel_id=1, replica_groups=mesh['row'=8,'col'=4] {'col'}, dimensions={1}, use_global_device_ids=true | all-gather | bytes 491520 | tf_op jit(solution)/shard_map/all_gather | solution.py:49
  38.1 45.3 %all_gather.19 = bf16[256,48,32]{1,2,0:T(8,128)(2,1)S(1)} all-gather(bf16[32,48,32]{1,2,0:T(8,128)(2,1)S(1)} %fusion.17), channel_id=1, replica_groups=mesh['row'=8,'col'=4] {'row'}, dimensions={0}, use_global_device_ids=true | all-gather | bytes 884736 | tf_op jit(solution)/shard_map/all_gather | solution.py:45
  83.6 3.8 %reshape.108 = bf16[8,2,12288]{2,1,0:T(2,128)(2,1)} reshape(bf16[192,32,32]{2,1,0:T(8,128)(2,1)} %bitcast.89) | data formatting | bytes 786432
  87.4 2.4 copy.56
  89.8 3.6 %all-to-all-start = ((bf16[8,2,12288]{2,1,0:T(2,128)(2,1)}), bf16[8,2,12288]{2,1,0:T(2,128)(2,1)S(1)}, u32[]{:S(2)}, u32[]{:S(2)}) async-start(bf16[8,2,12288]{2,1,0:T(2,128)(2,1)} %reshape.108), calls=%async_computation | async-start | bytes 786432 | tf_op jit(solution)/shard_map/all_to_all | solution.py:53
  93.4 35.2 %all_gather.21 = bf16[256,48]{1,0:T(8,128)(2,1)S(1)} all-gather(bf16[32,48]{1,0:T(8,128)(2,1)S(1)} %get-tuple-element.7), channel_id=1, replica_groups=mesh['row'=8,'col'=4] {'row'}, dimensions={0}, use_global_device_ids=true | all-gather | bytes 27648 | tf_op jit(solution)/shard_map/all_gather | solution.py:46
  131.6 3.7 %convert_bitcast_fusion = bf16[24,48,32,32]{1,2,3,0:T(8,128)(2,1)} fusion(bf16[24,32,256,1]{2,1,3,0:T(8,128)(2,1)S(1)} %bitcast.90, bf16[48,32,256]{2,0,1:T(8,128)(2,1)S(1)} %copy-done.4), kind=kOutput, calls=%fused_computation | convolution fusion | flops 605159424 | bytes 3538944 | tf_op jit(solution)/shard_map/dot_general | solution.py:58
  135.3 17.8 %copy.57 = bf16[24,48,32,32]{3,2,1,0:T(8,128)(2,1)} copy(bf16[24,48,32,32]{1,2,3,0:T(8,128)(2,1)} %convert_bitcast_fusion) | data formatting | bytes 4718592 | tf_op jit(solution)/shard_map/convert_element_type | solution.py:67
  153.1 12.7 %reshape.95 = bf16[24,48,1024]{2,1,0:T(8,128)(2,1)S(1)} reshape(bf16[24,48,32,32]{3,2,1,0:T(8,128)(2,1)} %copy.57) | data formatting | bytes 4718592 | tf_op jit(solution)/shard_map/reshape | solution.py:69
  165.9 1.8 fusion.49
  168.7 1.2 fusion.22
  170.7 48.0 %all-gather.4.cloned.1.call-done = bf16[192,48,128]{2,1,0:T(8,128)(2,1)} async-done(((bf16[24,48,128]{2,1,0:T(8,128)(2,1)}), bf16[192,48,128]{2,1,0:T(8,128)(2,1)}) %all-gather.4.cloned.1.call-update) | async-done | bytes 2359312 | tf_op jit(solution)/shard_map/all_gather | solution.py:92
  218.7 3.9 %all-to-all-start.2 = ((bf16[192,48,128]{2,1,0:T(8,128)(2,1)}), bf16[192,48,128]{2,1,0:T(8,128)(2,1)S(1)}, u32[]{:S(2)}, u32[]{:S(2)}) async-start(bf16[192,48,128]{2,1,0:T(8,128)(2,1)} %all-gather.4.cloned.1.call-done), calls=%async_computation.2 | async-start | bytes 4718592 | tf_op jit(solution)/shard_map/all_to_all | solution.py:93
  222.6 1.3 fusion.9
  223.9 18.8 %all-gather.6.cloned.1.call-done = bf16[24,192,128]{2,1,0:T(8,128)(2,1)} async-done(((bf16[24,48,128]{2,1,0:T(8,128)(2,1)}), bf16[24,192,128]{2,1,0:T(8,128)(2,1)}) %all-gather.6.cloned.1.call-update) | async-done | bytes 1179664 | tf_op jit(solution)/shard_map/all_gather | solution.py:96
  242.7 2.8 %copy.63 = bf16[24,192,128]{1,0,2:T(8,128)(2,1)} copy(bf16[24,192,128]{2,1,0:T(8,128)(2,1)} %all-gather.6.cloned.1.call-done) | data formatting | bytes 2359296 | tf_op jit(solution)/shard_map/all_gather | solution.py:96
  245.5 11.6 %all-to-all-done.2 = bf16[192,48,128]{2,1,0:T(8,128)(2,1)S(1)} async-done(((bf16[192,48,128]{2,1,0:T(8,128)(2,1)}), bf16[192,48,128]{2,1,0:T(8,128)(2,1)S(1)}, u32[]{:S(2)}, u32[]{:S(2)}) %all-to-all-start.2) | async-done | bytes 2359328 | tf_op jit(solution)/shard_map/all_to_all | solution.py:93
  257.1 2.1 copy.61
  259.2 3.8 %copy.62 = bf16[48,192,128]{1,0,2:T(8,128)(2,1)S(1)} copy(bf16[48,192,128]{2,1,0:T(8,128)(2,1)} %bitcast.86) | data formatting | bytes 4718592 | tf_op jit(solution)/shard_map/all_to_all | solution.py:93
  263.0 2.4 bitcast_reduce_fusion
  267.8 1.5 fusion.15
  (69 shorter events, 11.6 us)
Async XLA Ops:
  6.5 159.3 %copy-start = (bf16[1024,128]{1,0:T(8,128)(2,1)S(1)}, bf16[1024,128]{1,0:T(8,128)(2,1)}, u32[]{:S(2)}) copy-start(bf16[1024,128]{1,0:T(8,128)(2,1)} %param.18) | copy-start | bytes 786436
  6.5 15.7 %copy-start.3 = (bf16[32,48,256]{2,1,0:T(8,128)(2,1)S(1)}, bf16[32,48,256]{2,1,0:T(8,128)(2,1)}, u32[]{:S(2)}) copy-start(bf16[32,48,256]{2,1,0:T(8,128)(2,1)} %param.12) | copy-start | bytes 2359300
  6.5 16.2 %copy-start.11 = (bf16[256,32]{0,1:T(8,128)(2,1)S(1)}, bf16[256,32]{0,1:T(8,128)(2,1)}, u32[]{:S(2)}) copy-start(bf16[256,32]{0,1:T(8,128)(2,1)} %param.16) | copy-start | bytes 49156
  14.5 75.3 %all-to-all-start.1 = ((bf16[8,2,384]{2,1,0:T(2,128)(2,1)}), bf16[8,2,384]{2,1,0:T(2,128)(2,1)S(1)}, u32[]{:S(2)}, u32[]{:S(2)}) async-start(bf16[8,2,384]{2,1,0:T(2,128)(2,1)} %reshape.110), calls=%async_computation.1 | async-start | bytes 24576 | tf_op jit(solution)/shard_map/all_to_all | solution.py:54
  23.4 14.0 %copy-start.12 = (bf16[256,32]{0,1:T(8,128)(2,1)S(1)}, bf16[256,32]{0,1:T(8,128)(2,1)}, u32[]{:S(2)}) copy-start(bf16[256,32]{0,1:T(8,128)(2,1)} %param.17) | copy-start | bytes 49156
  38.1 45.4 %copy-start.13 = (s32[192]{0:T(256)S(1)}, s32[192]{0:T(256)}, u32[]{:S(2)}) copy-start(s32[192]{0:T(256)} %param.14) | copy-start | bytes 2308
  89.8 39.2 %all-to-all-start = ((bf16[8,2,12288]{2,1,0:T(2,128)(2,1)}), bf16[8,2,12288]{2,1,0:T(2,128)(2,1)S(1)}, u32[]{:S(2)}, u32[]{:S(2)}) async-start(bf16[8,2,12288]{2,1,0:T(2,128)(2,1)} %reshape.108), calls=%async_computation | async-start | bytes 786432 | tf_op jit(solution)/shard_map/all_to_all | solution.py:53
  93.4 125.3 %all-gather.4.cloned.1.call-start = ((), (), s32[]{:S(2)}) async-start(), calls=%async_computation.3 | async-start | bytes 2654208 | tf_op jit(solution)/shard_map/all_gather | solution.py:92
  130.4 1.2 copy-start.4
  165.9 2.3 copy-start.6
  167.7 54.8 %copy-start.1 = (f32[24,48,128]{2,1,0:T(8,128)}, f32[24,48,128]{2,1,0:T(8,128)S(1)}, u32[]{:S(2)}) copy-start(f32[24,48,128]{2,1,0:T(8,128)S(1)} %get-tuple-element.10) | copy-start | bytes 1769476
  169.9 72.8 %all-gather.6.cloned.1.call-start = ((), (), s32[]{:S(2)}) async-start(), calls=%async_computation.4 | async-start | bytes 1474560 | tf_op jit(solution)/shard_map/all_gather | solution.py:96
  170.7 51.9 %copy-start.10 = (bf16[128,128]{1,0:T(8,128)(2,1)S(1)}, bf16[128,128]{1,0:T(8,128)(2,1)}, u32[]{:S(2)}) copy-start(bf16[128,128]{1,0:T(8,128)(2,1)} %param.20) | copy-start | bytes 98308
  218.7 38.4 %all-to-all-start.2 = ((bf16[192,48,128]{2,1,0:T(8,128)(2,1)}), bf16[192,48,128]{2,1,0:T(8,128)(2,1)S(1)}, u32[]{:S(2)}, u32[]{:S(2)}) async-start(bf16[192,48,128]{2,1,0:T(8,128)(2,1)} %all-gather.4.cloned.1.call-done), calls=%async_computation.2 | async-start | bytes 4718592 | tf_op jit(solution)/shard_map/all_to_all | solution.py:93
  265.6 1.1 copy-start.2
  265.6 1.2 copy-start.5
  265.6 1.2 copy-start.7
  266.9 0.9 copy-start.8
  266.9 1.0 copy-start.9
Sparse Core Ops, SparseCore 0:
  170.0 48.6 all-gather.3
  220.2 22.3 all-gather.5
where the time goes:
time: 277 us; the launch traced here: 276 us
  blocking collectives  100 us (36%)
  waiting for transfers between devices  79.1 us (29%)
  local copies, waits for them, and re-layouts  50.8 us (18%)
  starting transfers between devices  13.7 us (5%)
  between operations  13.7 us (5%)
  matrix products  13.2 us (5%)
  other arithmetic  5.45 us (2%)
    all_gather x1, waiting for transfers between devices, shards(): right_cols = lax.all_gather(right_tri, 'row', axis=0, tiled=True)  48 us
    all_gather x1, blocking collectives, shards(): lax.all_gather(right_side, 'row', axis=0, tiled=True)  45.3 us
    all_gather x1, blocking collectives, shards(): lax.all_gather(mask_wire, 'row', axis=0, tiled=True)  35.2 us
    all_gather x1, waiting for transfers between devices, shards(): lax.all_gather(left_tri, 'col', axis=1, tiled=True)  18.8 us
    convert_element_type x1, local copies, waits for them, and re-layouts, shards(): outer = outer.reshape(block_rows, narrow, block_cols, narrow).transpose(0...  17.8 us
    all_gather x1, blocking collectives, shards(): lax.all_gather(left_side, 'col', axis=1, tiled=True)  13.4 us
    reshape x1, local copies, waits for them, and re-layouts, shards(): outer = outer.reshape(block_rows, block_cols, narrow * narrow)  12.7 us
    all_to_all x1, waiting for transfers between devices, shards(): lax.all_to_all(right_cols, 'col', split_axis=0, concat_axis=1, tiled=True)  11.6 us
  transfers between devices with their start and end apart: 5, of which 3 were waited for; matrix products, arithmetic and copies ran while one was open for 5% of the time, Pallas kernels for 0%

commit v1 on v0

--- a/solution.py
+++ b/solution.py
@@ -91,12 +91,37 @@
     ).astype(jnp.bfloat16)
     right_cols = lax.all_gather(right_tri, "row", axis=0, tiled=True)
     right_rows = lax.all_to_all(right_cols, "col", split_axis=0, concat_axis=1, tiled=True)
+    devices, index, rows = (lax.axis_size("col"), lax.axis_index("col"), left_tri.shape[1])
+    right = [(i, (i + 1) % devices) for i in range(devices)]
+    left = [(i, (i - 1) % devices) for i in range(devices)]
+    half = devices // 2
+    from_left = from_right = left_tri
     summed = jnp.einsum(
         "ikc,jkc->ijc",
-        lax.all_gather(left_tri, "col", axis=1, tiled=True),
-        right_rows,
+        left_tri,
+        lax.dynamic_slice_in_dim(right_rows, index * rows, left_tri.shape[1], axis=1),
         preferred_element_type=jnp.float32,
     )
+    for step in range(1, half + 1):
+        from_left = lax.ppermute(from_left, "col", right)
+        if step < devices - half:
+            from_right = lax.ppermute(from_right, "col", left)
+            summed = summed + jnp.einsum(
+                "ikc,jkc->ijc",
+                from_right,
+                lax.dynamic_slice_in_dim(
+                    right_rows, (index + step) % devices * rows, from_right.shape[1], axis=1
+                ),
+                preferred_element_type=jnp.float32,
+            )
+        summed = summed + jnp.einsum(
+            "ikc,jkc->ijc",
+            from_left,
+            lax.dynamic_slice_in_dim(
+                right_rows, (index - step) % devices * rows, from_left.shape[1], axis=1
+            ),
+            preferred_element_type=jnp.float32,
+        )
     normed_sum = normalize(summed).astype(jnp.bfloat16)
     update = jax.nn.sigmoid(
         jnp.dot(normed_pair, triangle_gate, preferred_element_type=jnp.float32)

time: 277 us -> 293 us (1.058)
  local copies, waits for them, and re-layouts: 50.8 us -> 58.8 us
  matrix products: 13.2 us -> 17.1 us
    ppermute x0 -> x3, waiting for transfers between devices: none -> 32.5 us  [the longest x2 32.5 us: shards(): from_left = lax.ppermute(from_left, 'col', right)]
    all_gather x1 -> x0, waiting for transfers between devices: 18.8 us -> none  [shards(): lax.all_gather(left_tri, 'col', axis=1, tiled=True)]
    all_to_all x1, waiting for transfers between devices: 11.6 us -> 0.01 us  [shards(): lax.all_to_all(right_cols, 'col', split_axis=0, concat_axis=1, tiled=True)]
    unnamed x33 -> x43, local copies, waits for them, and re-layouts: 6.54 us -> 13.2 us
    ppermute x0 -> x3, local copies, waits for them, and re-layouts: none -> 6.63 us  [the longest x2 4.42 us: shards(): from_left = lax.ppermute(from_left, 'col', right)]
    all_to_all x2 -> x1, local copies, waits for them, and re-layouts: 5.89 us -> 0.71 us  [shards(): lax.all_to_all(right_cols, 'col', split_axis=0, concat_axis=1, tiled=True)]
    dot_general x1 -> x4, matrix products: 2.35 us -> 5.48 us  [the longest x1 2.67 us: shards(): jnp.einsum('ikc,jkc->ijc', from_right, lax.dynamic_slice_in_dim(right_row...]
  transfers between devices with their start and end apart: 5 -> 7, of which waited for: 3 -> 2; matrix products, arithmetic and copies ran while one was open for 5% -> 7% of each run, Pallas kernels for 0% -> 0%
where the time goes in v1:
time: 293 us; the launch traced here: 292 us
  blocking collectives  100 us (34%)
  waiting for transfers between devices  81.3 us (28%)
  local copies, waits for them, and re-layouts  58.8 us (20%)
  matrix products  17.1 us (6%)
  starting transfers between devices  15.3 us (5%)
  between operations  13.8 us (5%)
  other arithmetic  5.36 us (2%)
    all_gather x1, waiting for transfers between devices, shards(): right_cols = lax.all_gather(right_tri, 'row', axis=0, tiled=True)  48.8 us
    all_gather x1, blocking collectives, shards(): lax.all_gather(right_side, 'row', axis=0, tiled=True)  45.3 us
    all_gather x1, blocking collectives, shards(): lax.all_gather(mask_wire, 'row', axis=0, tiled=True)  35.2 us
    ppermute x2, waiting for transfers between devices, shards(): from_left = lax.ppermute(from_left, 'col', right)  32.5 us
    convert_element_type x1, local copies, waits for them, and re-layouts, shards(): outer = outer.reshape(block_rows, narrow, block_cols, narrow).transpose(0...  17.8 us
    all_gather x1, blocking collectives, shards(): lax.all_gather(left_side, 'col', axis=1, tiled=True)  13.4 us
    unnamed x43, local copies, waits for them, and re-layouts  13.2 us
    reshape x1, local copies, waits for them, and re-layouts, shards(): outer = outer.reshape(block_rows, block_cols, narrow * narrow)  12.7 us
  transfers between devices with their start and end apart: 7, of which 2 were waited for; matrix products, arithmetic and copies ran while one was open for 7% of the time, Pallas kernels for 0%

profile of v1, /device:TPU:0, one launch (start us, length us, event | category | flops | bytes accessed | tf_op | source)
XLA Modules:
  0.0 291.7 jit_solution(12543676203472864745)
XLA Ops:
  7.4 6.2 %all-gather = bf16[4,48,32]{1,2,0:T(8,128)(2,1)S(1)} all-gather(bf16[1,48,32]{1,2,0:T(8,128)(2,1)S(1)} %bitcast.99), channel_id=1, replica_groups=mesh['row'=8,'col'=4] {'col'}, dimensions={0}, use_global_device_ids=true | all-gather | bytes 15360 | tf_op jit(solution)/shard_map/all_gather | solution.py:50
  14.5 6.2 %all-to-all-start.1 = ((bf16[8,2,384]{2,1,0:T(2,128)(2,1)}), bf16[8,2,384]{2,1,0:T(2,128)(2,1)S(1)}, u32[]{:S(2)}, u32[]{:S(2)}) async-start(bf16[8,2,384]{2,1,0:T(2,128)(2,1)} %reshape.110), calls=%async_computation.1 | async-start | bytes 24576 | tf_op jit(solution)/shard_map/all_to_all | solution.py:54
  24.1 13.4 %all_gather.15 = bf16[32,192,32]{2,0,1:T(8,128)(2,1)} all-gather(bf16[32,48,32]{2,0,1:T(8,128)(2,1)S(1)} %copy.72), channel_id=1, replica_groups=mesh['row'=8,'col'=4] {'col'}, dimensions={1}, use_global_device_ids=true | all-gather | bytes 491520 | tf_op jit(solution)/shard_map/all_gather | solution.py:49
  38.1 45.3 %all_gather.16 = bf16[256,48,32]{1,2,0:T(8,128)(2,1)S(1)} all-gather(bf16[32,48,32]{1,2,0:T(8,128)(2,1)S(1)} %fusion.17), channel_id=1, replica_groups=mesh['row'=8,'col'=4] {'row'}, dimensions={0}, use_global_device_ids=true | all-gather | bytes 884736 | tf_op jit(solution)/shard_map/all_gather | solution.py:45
  83.6 3.8 %reshape.108 = bf16[8,2,12288]{2,1,0:T(2,128)(2,1)} reshape(bf16[192,32,32]{2,1,0:T(8,128)(2,1)} %bitcast.95) | data formatting | bytes 786432
  87.4 2.4 copy.77
  89.8 3.6 %all-to-all-start = ((bf16[8,2,12288]{2,1,0:T(2,128)(2,1)}), bf16[8,2,12288]{2,1,0:T(2,128)(2,1)S(1)}, u32[]{:S(2)}, u32[]{:S(2)}) async-start(bf16[8,2,12288]{2,1,0:T(2,128)(2,1)} %reshape.108), calls=%async_computation | async-start | bytes 786432 | tf_op jit(solution)/shard_map/all_to_all | solution.py:53
  93.4 35.2 %all_gather.18 = bf16[256,48]{1,0:T(8,128)(2,1)S(1)} all-gather(bf16[32,48]{1,0:T(8,128)(2,1)S(1)} %get-tuple-element.11), channel_id=1, replica_groups=mesh['row'=8,'col'=4] {'row'}, dimensions={0}, use_global_device_ids=true | all-gather | bytes 27648 | tf_op jit(solution)/shard_map/all_gather | solution.py:46
  131.6 3.7 %convert_bitcast_fusion = bf16[24,48,32,32]{1,2,3,0:T(8,128)(2,1)} fusion(bf16[24,32,256,1]{2,1,3,0:T(8,128)(2,1)S(1)} %bitcast.96, bf16[48,32,256]{2,0,1:T(8,128)(2,1)S(1)} %copy-done.5), kind=kOutput, calls=%fused_computation | convolution fusion | flops 605159424 | bytes 3538944 | tf_op jit(solution)/shard_map/dot_general | solution.py:58
  135.3 17.8 %copy.78 = bf16[24,48,32,32]{3,2,1,0:T(8,128)(2,1)} copy(bf16[24,48,32,32]{1,2,3,0:T(8,128)(2,1)} %convert_bitcast_fusion) | data formatting | bytes 4718592 | tf_op jit(solution)/shard_map/convert_element_type | solution.py:67
  153.1 12.7 %reshape.95 = bf16[24,48,1024]{2,1,0:T(8,128)(2,1)S(1)} reshape(bf16[24,48,32,32]{3,2,1,0:T(8,128)(2,1)} %copy.78) | data formatting | bytes 4718592 | tf_op jit(solution)/shard_map/reshape | solution.py:69
  165.9 1.8 fusion.49
  169.8 48.8 %all-gather.3.cloned.1.call-done = bf16[192,48,128]{2,1,0:T(8,128)(2,1)} async-done(((bf16[24,48,128]{2,1,0:T(8,128)(2,1)}), bf16[192,48,128]{2,1,0:T(8,128)(2,1)}) %all-gather.3.cloned.1.call-update) | async-done | bytes 2359312 | tf_op jit(solution)/shard_map/all_gather | solution.py:92
  218.6 3.6 %all-to-all-start.2 = ((bf16[192,48,128]{2,1,0:T(8,128)(2,1)}), bf16[192,48,128]{2,1,0:T(8,128)(2,1)S(1)}, u32[]{:S(2)}, u32[]{:S(2)}) async-start(bf16[192,48,128]{2,1,0:T(8,128)(2,1)} %all-gather.3.cloned.1.call-done), calls=%async_computation.2 | async-start | bytes 4718592 | tf_op jit(solution)/shard_map/all_to_all | solution.py:93
  224.0 32.5 %collective-permute-done.1 = bf16[24,48,128]{2,1,0:T(8,128)(2,1)} collective-permute-done((bf16[24,48,128]{2,1,0:T(8,128)(2,1)S(1)}, bf16[24,48,128]{2,1,0:T(8,128)(2,1)}, u32[]{:S(2)}, u32[]{:S(2)}) %collective-permute-start.1) | collective-permute-done | bytes 294944 | tf_op jit(solution)/shard_map/ppermute | solution.py:106
  257.8 2.1 fusion.9
  259.9 2.2 copy.88
  262.1 2.2 copy.86
  264.3 2.2 copy.90
  268.6 1.7 copy.98
  270.3 1.8 copy.97
  273.0 1.8 copy.100
  274.9 2.7 fusion.52
  283.3 1.5 fusion.15
  (88 shorter events, 22.6 us)
Async XLA Ops:
  6.5 159.3 %copy-start = (bf16[1024,128]{1,0:T(8,128)(2,1)S(1)}, bf16[1024,128]{1,0:T(8,128)(2,1)}, u32[]{:S(2)}) copy-start(bf16[1024,128]{1,0:T(8,128)(2,1)} %param.18) | copy-start | bytes 786436
  6.5 15.7 %copy-start.4 = (bf16[32,48,256]{2,1,0:T(8,128)(2,1)S(1)}, bf16[32,48,256]{2,1,0:T(8,128)(2,1)}, u32[]{:S(2)}) copy-start(bf16[32,48,256]{2,1,0:T(8,128)(2,1)} %param.12) | copy-start | bytes 2359300
  6.5 16.2 %copy-start.14 = (bf16[256,32]{0,1:T(8,128)(2,1)S(1)}, bf16[256,32]{0,1:T(8,128)(2,1)}, u32[]{:S(2)}) copy-start(bf16[256,32]{0,1:T(8,128)(2,1)} %param.16) | copy-start | bytes 49156
  14.5 75.2 %all-to-all-start.1 = ((bf16[8,2,384]{2,1,0:T(2,128)(2,1)}), bf16[8,2,384]{2,1,0:T(2,128)(2,1)S(1)}, u32[]{:S(2)}, u32[]{:S(2)}) async-start(bf16[8,2,384]{2,1,0:T(2,128)(2,1)} %reshape.110), calls=%async_computation.1 | async-start | bytes 24576 | tf_op jit(solution)/shard_map/all_to_all | solution.py:54
  23.4 14.0 %copy-start.15 = (bf16[256,32]{0,1:T(8,128)(2,1)S(1)}, bf16[256,32]{0,1:T(8,128)(2,1)}, u32[]{:S(2)}) copy-start(bf16[256,32]{0,1:T(8,128)(2,1)} %param.17) | copy-start | bytes 49156
  38.1 45.4 %copy-start.16 = (s32[192]{0:T(256)S(1)}, s32[192]{0:T(256)}, u32[]{:S(2)}) copy-start(s32[192]{0:T(256)} %param.14) | copy-start | bytes 2308
  89.8 39.2 %all-to-all-start = ((bf16[8,2,12288]{2,1,0:T(2,128)(2,1)}), bf16[8,2,12288]{2,1,0:T(2,128)(2,1)S(1)}, u32[]{:S(2)}, u32[]{:S(2)}) async-start(bf16[8,2,12288]{2,1,0:T(2,128)(2,1)} %reshape.108), calls=%async_computation | async-start | bytes 786432 | tf_op jit(solution)/shard_map/all_to_all | solution.py:53
  93.4 125.2 %all-gather.3.cloned.1.call-start = ((), (), s32[]{:S(2)}) async-start(), calls=%async_computation.3 | async-start | bytes 2654208 | tf_op jit(solution)/shard_map/all_gather | solution.py:92
  130.4 1.2 copy-start.5
  165.9 2.3 copy-start.10
  167.7 90.1 %copy-start.2 = (f32[24,48,128]{2,1,0:T(8,128)}, f32[24,48,128]{2,1,0:T(8,128)S(1)}, u32[]{:S(2)}) copy-start(f32[24,48,128]{2,1,0:T(8,128)S(1)} %get-tuple-element.14) | copy-start | bytes 1769476
  218.6 47.9 %all-to-all-start.2 = ((bf16[192,48,128]{2,1,0:T(8,128)(2,1)}), bf16[192,48,128]{2,1,0:T(8,128)(2,1)S(1)}, u32[]{:S(2)}, u32[]{:S(2)}) async-start(bf16[192,48,128]{2,1,0:T(8,128)(2,1)} %all-gather.3.cloned.1.call-done), calls=%async_computation.2 | async-start | bytes 4718592 | tf_op jit(solution)/shard_map/all_to_all | solution.py:93
  222.2 34.3 %collective-permute-start.1 = (bf16[24,48,128]{2,1,0:T(8,128)(2,1)S(1)}, bf16[24,48,128]{2,1,0:T(8,128)(2,1)}, u32[]{:S(2)}, u32[]{:S(2)}) collective-permute-start(bf16[24,48,128]{2,1,0:T(8,128)(2,1)S(1)} %get-tuple-element.5), channel_id=1, source_target_pairs={{0,1},{1,2},{2,3},{3,0},{4,5},{5,6},{6,7},{7,4},{8,9},{9,10},{10,1... | collective-permute-start | bytes 884744 | tf_op jit(solution)/shard_map/ppermute | solution.py:106
  222.7 39.4 %collective-permute-start = (bf16[24,48,128]{2,1,0:T(8,128)(2,1)S(1)}, bf16[24,48,128]{2,1,0:T(8,128)(2,1)}, u32[]{:S(2)}, u32[]{:S(2)}) collective-permute-start(bf16[24,48,128]{2,1,0:T(8,128)(2,1)S(1)} %get-tuple-element.5), channel_id=1, source_target_pairs={{0,3},{1,0},{2,1},{3,2},{4,7},{5,4},{6,5},{7,6},{8,11},{9,8},{10,9... | collective-permute-start | bytes 884744 | tf_op jit(solution)/shard_map/ppermute | solution.py:108
  256.5 7.8 %collective-permute-start.2 = (bf16[24,48,128]{2,1,0:T(8,128)(2,1)}, bf16[24,48,128]{2,1,0:T(8,128)(2,1)}, u32[]{:S(2)}, u32[]{:S(2)}) collective-permute-start(bf16[24,48,128]{2,1,0:T(8,128)(2,1)} %collective-permute-done.1), channel_id=1, source_target_pairs={{0,1},{1,2},{2,3},{3,0},{4,5},{5,6},{6,7},{7,4},{8,9},{9,10},{10,1... | collective-permute-start | bytes 884744 | tf_op jit(solution)/shard_map/ppermute | solution.py:106
  274.9 2.7 copy-start.1
  274.9 2.7 copy-start.7
  277.6 1.1 copy-start.8
  278.7 1.1 copy-start.6
  281.1 1.1 copy-start.3
  281.1 1.2 copy-start.9
  281.1 1.2 copy-start.11
  282.4 0.9 copy-start.12
  282.4 1.0 copy-start.13
Sparse Core Ops, SparseCore 0:
  169.9 48.6 all-gather.2
